TPU v7x, 32 devices: a whole 2x2x4 slice. The times are simulated.
32 devices in a mesh: dp: 8 (over z, x), tensor: 4 (over y, core).
Axes of the slice: x: 2, y: 2, z: 4, core: 2. Of those that a mesh axis runs over, the one named last changes fastest.
Arguments:
- tokens: bfloat16 [8192, 1024], P(('dp', 'tensor')), may hold values from -6 to 6
- attn_gain: float32 [1024], replicated, may hold values from 0.5 to 1.5
- qkv_weight: bfloat16 [1024, 16, 192], P('dp', 'tensor'), may hold values from -0.1875 to 0.1875
- out_weight: bfloat16 [1024, 1024], P('tensor', 'dp'), may hold values from -4 to 4
- mlp_gain: float32 [1024], replicated, may hold values from 0.5 to 1.5
- in_weight: bfloat16 [1024, 2, 2624], P('dp', None, 'tensor'), may hold values from -0.1875 to 0.1875
- down_weight: bfloat16 [2624, 1024], P('tensor', 'dp'), may hold values from -0.125 to 0.125
- seg_lengths: int32 [8, 3], P('dp'), may hold values from 1 to 512, 1024 in all within a row
- cotangent: bfloat16 [8192, 1024], P(('dp', 'tensor')), may hold values from -12 to 12
Outputs:
- layer_out: bfloat16 [8192, 1024], P(('dp', 'tensor'))
- grad_tokens: bfloat16 [8192, 1024], P(('dp', 'tensor'))
- grad_attn_gain: float32 [1024], replicated
- grad_qkv_weight: float32 [1024, 16, 192], P('dp', 'tensor')
- grad_out_weight: float32 [1024, 1024], P('tensor', 'dp')
- grad_mlp_gain: float32 [1024], replicated
- grad_in_weight: float32 [1024, 2, 2624], P('dp', None, 'tensor')
- grad_down_weight: float32 [2624, 1024], P('tensor', 'dp')
Inputs may be any that keep to these rules, and one draw needn't show every extreme that they name: `seg_lengths`: row p holds the lengths of the 3 segments that fill pack p in order; they sum to 1024 and the longest is 512.
All inputs are finite; a program needn't handle non-finite values.
Results may differ from a plain program's by a relative error of at most 0.024.
Values may be sent and summed in bfloat16 or wider, within the bound.
A program may use at most 128 MiB of HBM per device.

v0:
```python
import math
import jax
import jax.numpy as jnp
from jax import lax
from jax.sharding import PartitionSpec as P

NORM_EPS = 1e-05
ROPE_BASE = 160000.0
HALF_ROOT = 0.7071067811865476
INV_ROOT_TAU = 0.3989422804014327
MASKED_SCORE = -1e30


def dot_plain(left, right):
    return jnp.dot(left, right, preferred_element_type=jnp.float32)


def dot_first(left, right):
    return lax.dot_general(
        left, right, (((0,), (0,)), ((), ())), preferred_element_type=jnp.float32
    )


def dot_last(left, right):
    return lax.dot_general(
        left, right, (((1,), (1,)), ((), ())), preferred_element_type=jnp.float32
    )


def layer_norm(row_data, norm_gain):
    centered = row_data - jnp.mean(row_data, axis=-1, keepdims=True)
    inverse = lax.rsqrt(jnp.mean(centered * centered, axis=-1, keepdims=True) + NORM_EPS)
    unit_rows = centered * inverse
    return (unit_rows * norm_gain, unit_rows, inverse)


def norm_back(grad_normed, unit_rows, inverse, norm_gain):
    scaled = grad_normed * norm_gain
    grad_rows = inverse * (
        scaled
        - jnp.mean(scaled, axis=-1, keepdims=True)
        - unit_rows * jnp.mean(scaled * unit_rows, axis=-1, keepdims=True)
    )
    return (grad_rows, jnp.sum(grad_normed * unit_rows, axis=0))


def gelu_parts(value_in):
    normal_cdf = 0.5 * (1.0 + lax.erf(value_in * HALF_ROOT))
    slope = normal_cdf + value_in * INV_ROOT_TAU * jnp.exp(-0.5 * value_in * value_in)
    return (value_in * normal_cdf, slope)


def segment_info(seg_lens, pack_rows):
    seg_ends = jnp.cumsum(seg_lens)
    places = lax.iota(jnp.int32, pack_rows)
    before = seg_ends[None, :] <= places[:, None]
    seg_ids = jnp.sum(before.astype(jnp.int32), axis=1)
    seg_first = jnp.sum(jnp.where(before, seg_lens[None, :], 0), axis=1)
    return (seg_ids, places - seg_first)


def rotary(position, head_dim):
    half_dim = head_dim // 2
    inv_freq = jnp.exp(lax.iota(jnp.float32, half_dim) * (-2.0 * math.log(ROPE_BASE) / head_dim))
    angles = position.astype(jnp.float32)[:, None] * inv_freq[None, :]
    return (jnp.cos(angles), jnp.sin(angles))


def turn(vectors, cos_table, sin_table):
    half_dim = vectors.shape[-1] // 2
    front_half = vectors[..., :half_dim]
    back_half = vectors[..., half_dim:]
    cos_part = cos_table[:, None, :]
    sin_part = sin_table[:, None, :]
    return jnp.concatenate(
        [
            front_half * cos_part - back_half * sin_part,
            back_half * cos_part + front_half * sin_part,
        ],
        axis=-1,
    )


def turn_back(grads_in, cos_table, sin_table):
    half_dim = grads_in.shape[-1] // 2
    front_half = grads_in[..., :half_dim]
    back_half = grads_in[..., half_dim:]
    cos_part = cos_table[:, None, :]
    sin_part = sin_table[:, None, :]
    return jnp.concatenate(
        [
            front_half * cos_part + back_half * sin_part,
            back_half * cos_part - front_half * sin_part,
        ],
        axis=-1,
    )


def block_scores(query_part, key_part, seg_query, seg_key, score_scale):
    scores = (
        jnp.einsum("qhd,khd->hqk", query_part, key_part, preferred_element_type=jnp.float32)
        * score_scale
    )
    return jnp.where((seg_query[:, None] == seg_key[None, :])[None], scores, MASKED_SCORE)


def attention_forward(query_rows, key_rows, value_rows, seg_ids, query_block, score_scale):
    pack_rows, heads_local, head_dim = query_rows.shape
    block_count = pack_rows // query_block

    def one_block(block_index):
        query_start = block_index * query_block
        query_part = lax.dynamic_slice_in_dim(query_rows, query_start, query_block, 0)
        seg_query = lax.dynamic_slice_in_dim(seg_ids, query_start, query_block, 0)
        scores = block_scores(query_part, key_rows, seg_query, seg_ids, score_scale)
        row_top = jnp.max(scores, axis=-1, keepdims=True)
        expo = jnp.exp(scores - row_top)
        row_total = jnp.sum(expo, axis=-1, keepdims=True)
        weights = (expo / row_total).astype(jnp.bfloat16)
        result = jnp.einsum("hqk,khd->qhd", weights, value_rows, preferred_element_type=jnp.float32)
        return (result, (row_top + jnp.log(row_total))[..., 0])

    results, log_totals = lax.map(one_block, jnp.arange(block_count, dtype=jnp.int32))
    return (results.reshape(pack_rows, heads_local, head_dim), log_totals)


def attention_backward(
    query_rows, key_rows, value_rows, grad_attended, log_totals, seg_ids, query_block, score_scale
):
    pack_rows, heads_local, head_dim = query_rows.shape
    block_count = pack_rows // query_block

    def block_step(running, block_index):
        grad_keys, grad_values = running
        query_start = block_index * query_block
        query_part = lax.dynamic_slice_in_dim(query_rows, query_start, query_block, 0)
        grad_part = lax.dynamic_slice_in_dim(grad_attended, query_start, query_block, 0)
        seg_query = lax.dynamic_slice_in_dim(seg_ids, query_start, query_block, 0)
        scores = block_scores(query_part, key_rows, seg_query, seg_ids, score_scale)
        probs = jnp.exp(scores - log_totals[block_index][..., None])
        grad_probs = jnp.einsum(
            "qhd,khd->hqk", grad_part, value_rows, preferred_element_type=jnp.float32
        )
        inner = jnp.sum(probs * grad_probs, axis=-1, keepdims=True)
        grad_scores = (probs * (grad_probs - inner)).astype(jnp.bfloat16) * score_scale
        grad_query_part = jnp.einsum(
            "hqk,khd->qhd", grad_scores, key_rows, preferred_element_type=jnp.float32
        )
        grad_key_part = jnp.einsum(
            "hqk,qhd->khd", grad_scores, query_part, preferred_element_type=jnp.float32
        )
        grad_value_part = jnp.einsum(
            "hqk,qhd->khd",
            probs.astype(jnp.bfloat16),
            grad_part,
            preferred_element_type=jnp.float32,
        )
        grad_keys = grad_keys + grad_key_part
        grad_values = grad_values + grad_value_part
        return ((grad_keys, grad_values), grad_query_part)

    empty_grad = jnp.zeros(query_rows.shape, jnp.float32)
    (grad_keys, grad_values), grad_queries = lax.scan(
        block_step, (empty_grad, empty_grad), jnp.arange(block_count, dtype=jnp.int32)
    )
    return (grad_queries.reshape(pack_rows, heads_local, head_dim), grad_keys, grad_values)


def body(
    tokens,
    attn_gain,
    qkv_weight,
    out_weight,
    mlp_gain,
    in_weight,
    down_weight,
    seg_lengths,
    cotangent,
):
    tok_dev, model_width = tokens.shape
    pack_rows = tok_dev * lax.axis_size("tensor")
    heads_local = qkv_weight.shape[1]
    head_dim = qkv_weight.shape[2] // 3
    hidden_local = in_weight.shape[2]
    score_scale = head_dim ** (-0.5)
    query_block = min(512, pack_rows)
    qkv_full, out_full, in_full, down_full = (
        lax.all_gather(qkv_weight, "dp", axis=0, tiled=True),
        lax.all_gather(out_weight, "dp", axis=1, tiled=True),
        lax.all_gather(in_weight, "dp", axis=0, tiled=True),
        lax.all_gather(down_weight, "dp", axis=1, tiled=True),
    )
    qkv_flat = qkv_full.reshape(model_width, heads_local * 3 * head_dim)
    seg_ids, position = segment_info(seg_lengths[0], pack_rows)
    cos_table, sin_table = rotary(position, head_dim)
    row_data = tokens.astype(jnp.float32)
    normed_attn, unit_attn, inverse_attn = layer_norm(row_data, attn_gain)
    attn_input = lax.all_gather(normed_attn.astype(jnp.bfloat16), "tensor", axis=0, tiled=True)
    mixed_proj = dot_plain(attn_input, qkv_flat).reshape(pack_rows, heads_local, 3, head_dim)
    query_rows = turn(mixed_proj[:, :, 0], cos_table, sin_table).astype(jnp.bfloat16)
    key_rows = turn(mixed_proj[:, :, 1], cos_table, sin_table).astype(jnp.bfloat16)
    value_rows = mixed_proj[:, :, 2].astype(jnp.bfloat16)
    attended, log_totals = attention_forward(
        query_rows, key_rows, value_rows, seg_ids, query_block, score_scale
    )
    attended = attended.reshape(pack_rows, heads_local * head_dim).astype(jnp.bfloat16)
    residual = row_data + lax.psum_scatter(
        dot_plain(attended, out_full).astype(jnp.bfloat16),
        "tensor",
        scatter_dimension=0,
        tiled=True,
    ).astype(jnp.float32)
    normed_mlp, unit_mlp, inverse_mlp = layer_norm(residual, mlp_gain)
    mlp_input = normed_mlp.astype(jnp.bfloat16)
    mlp_rows = lax.all_gather(mlp_input, "tensor", axis=0, tiled=True)
    in_flat = in_full.reshape(model_width, -1)
    lifted = dot_plain(mlp_rows, in_flat).reshape(pack_rows, 2, hidden_local)
    act_gelu, act_slope = gelu_parts(lifted[:, 0])
    activated = (act_gelu * lifted[:, 1]).astype(jnp.bfloat16)
    layer_out = (
        residual
        + lax.psum_scatter(
            dot_plain(activated, down_full).astype(jnp.bfloat16),
            "tensor",
            scatter_dimension=0,
            tiled=True,
        ).astype(jnp.float32)
    ).astype(jnp.bfloat16)
    cotangent_rows = lax.all_gather(cotangent, "tensor", axis=0, tiled=True)
    grad_act = dot_last(cotangent_rows, down_full)
    grad_lifted = jnp.concatenate(
        [grad_act * lifted[:, 1] * act_slope, grad_act * act_gelu], axis=1
    ).astype(jnp.bfloat16)
    grad_mlp_in = lax.psum_scatter(
        dot_last(grad_lifted, in_flat).astype(jnp.bfloat16),
        "tensor",
        scatter_dimension=0,
        tiled=True,
    ).astype(jnp.float32)
    grad_in_part = dot_first(mlp_rows, grad_lifted).reshape(in_full.shape)
    grad_down_part = dot_first(activated, cotangent_rows)
    grad_resid_norm, mlp_gain_part = norm_back(grad_mlp_in, unit_mlp, inverse_mlp, mlp_gain)
    grad_residual = cotangent.astype(jnp.float32) + grad_resid_norm
    grad_branch = lax.all_gather(grad_residual.astype(jnp.bfloat16), "tensor", axis=0, tiled=True)
    grad_out_part = dot_first(attended, grad_branch)
    grad_attended = (
        dot_last(grad_branch, out_full)
        .astype(jnp.bfloat16)
        .reshape(pack_rows, heads_local, head_dim)
    )
    grad_queries, grad_keys, grad_values = attention_backward(
        query_rows,
        key_rows,
        value_rows,
        grad_attended,
        log_totals,
        seg_ids,
        query_block,
        score_scale,
    )
    grad_mixed = jnp.stack(
        [
            turn_back(grad_queries, cos_table, sin_table),
            turn_back(grad_keys, cos_table, sin_table),
            grad_values,
        ],
        axis=2,
    )
    grad_mixed = grad_mixed.reshape(pack_rows, heads_local * 3 * head_dim).astype(jnp.bfloat16)
    grad_qkv_part = dot_first(attn_input, grad_mixed).reshape(qkv_full.shape)
    grad_attn_in = lax.psum_scatter(
        dot_last(grad_mixed, qkv_flat).astype(jnp.bfloat16),
        "tensor",
        scatter_dimension=0,
        tiled=True,
    ).astype(jnp.float32)
    grad_rows_attn, attn_gain_part = norm_back(grad_attn_in, unit_attn, inverse_attn, attn_gain)
    grad_tokens = (grad_residual + grad_rows_attn).astype(jnp.bfloat16)
    qkv_grad, out_grad, in_grad, down_grad = (
        lax.psum_scatter(
            grad_qkv_part.astype(jnp.bfloat16), "dp", scatter_dimension=0, tiled=True
        ).astype(jnp.float32),
        lax.psum_scatter(
            grad_out_part.astype(jnp.bfloat16), "dp", scatter_dimension=1, tiled=True
        ).astype(jnp.float32),
        lax.psum_scatter(
            grad_in_part.astype(jnp.bfloat16), "dp", scatter_dimension=0, tiled=True
        ).astype(jnp.float32),
        lax.psum_scatter(
            grad_down_part.astype(jnp.bfloat16), "dp", scatter_dimension=1, tiled=True
        ).astype(jnp.float32),
    )
    attn_gain_grad, mlp_gain_grad = lax.psum((attn_gain_part, mlp_gain_part), ("dp", "tensor"))
    return (
        layer_out,
        grad_tokens,
        attn_gain_grad,
        qkv_grad,
        out_grad,
        mlp_gain_grad,
        in_grad,
        down_grad,
    )


def solution(mesh):
    in_specs = (
        P(("dp", "tensor"), None),
        P(),
        P("dp", "tensor", None),
        P("tensor", "dp"),
        P(),
        P("dp", None, "tensor"),
        P("tensor", "dp"),
        P("dp", None),
        P(("dp", "tensor"), None),
    )
    out_specs = (
        P(("dp", "tensor"), None),
        P(("dp", "tensor"), None),
        P(),
        P("dp", "tensor", None),
        P("tensor", "dp"),
        P(),
        P("dp", None, "tensor"),
        P("tensor", "dp"),
    )
    return jax.shard_map(body, mesh=mesh, in_specs=in_specs, out_specs=out_specs, check_vma=False)
```

profile of v0, /device:TPU:0, one launch (start us, length us, event | category | flops | bytes accessed | tf_op | source)
XLA Modules:
  0.0 726.5 jit_solution(4247788537337748045)
XLA Ops:
  11.1 2.1 fusion.107
  13.6 30.7 %all_gather.26 = bf16[256,1024]{1,0:T(8,128)(2,1)S(1)} all-gather(bf16[256,128]{1,0:T(8,128)(2,1)S(1)} %copy-done.18), channel_id=1, replica_groups=mesh['dp'=8,'tensor'=4] {'dp'}, dimensions={1}, use_global_device_ids=true | all-gather | bytes 589824 | tf_op jit(solution)/shard_map/all_gather | solution.py:189
  44.9 16.9 %all-gather.10.cloned.1.call-done = bf16[1024,4,192]{0,2,1:T(8,128)(2,1)} async-done(((bf16[128,4,192]{0,2,1:T(8,128)(2,1)}), bf16[1024,4,192]{0,2,1:T(8,128)(2,1)}) %all-gather.10.cloned.1.call-update) | async-done | bytes 1572880 | tf_op jit(solution)/shard_map/all_gather | solution.py:188
  61.8 23.0 %all-gather.8.cloned.1.call-done = bf16[1024,1024]{1,0:T(8,128)(2,1)} async-done(((bf16[256,1024]{1,0:T(8,128)(2,1)}), bf16[1024,1024]{1,0:T(8,128)(2,1)}) %all-gather.8.cloned.1.call-update) | async-done | bytes 2097168 | tf_op jit(solution)/shard_map/all_gather | solution.py:198
  84.8 3.9 fusion.89
  89.4 19.1 %while.27 = (s32[]{:T(128)}, bf16[2,512,4,64]{1,3,2,0:T(8,128)(2,1)}, f32[2,4,512]{2,1,0:T(4,128)S(1)}, s32[2]{0:T(128)S(1)}, s32[1024]{0:T(1024)S(1)}, /*index=...) while((s32[]{:T(128)}, ...), condition=%wide.region_8.9_spmd, body=%wide.region_5.8_spmd.sunk | while | flops 562558976 | bytes 33368320 | solution.py:123
  92.8 2.3 fusion.173
  95.2 3.0 fusion.174
  102.4 2.3 fusion.173
  104.7 3.0 fusion.174
  113.8 30.9 %reduce-scatter.17.cloned.1.call-done = bf16[256,1024]{1,0:T(8,128)(2,1)} async-done(((bf16[1024,1024]{1,0:T(8,128)(2,1)}), bf16[256,1024]{1,0:T(8,128)(2,1)}) %reduce-scatter.17.cloned.1.call-update) | async-done | bytes 524304 | tf_op jit(solution)/shard_map/reduce_scatter | solution.py:207
  151.3 53.2 %all-gather.14.cloned.1.call-done = bf16[1024,2,656]{0,2,1:T(8,128)(2,1)} async-done(((bf16[128,2,656]{0,2,1:T(8,128)(2,1)}), bf16[1024,2,656]{0,2,1:T(8,128)(2,1)}) %all-gather.14.cloned.1.call-update) | async-done | bytes 2686992 | tf_op jit(solution)/shard_map/all_gather | solution.py:190
  204.5 22.9 %all-gather.12.cloned.1.call-done = bf16[1024,1024]{1,0:T(8,128)(2,1)} async-done(((bf16[256,1024]{1,0:T(8,128)(2,1)}), bf16[1024,1024]{1,0:T(8,128)(2,1)}) %all-gather.12.cloned.1.call-update) | async-done | bytes 2097168 | tf_op jit(solution)/shard_map/all_gather | solution.py:215
  227.3 7.7 %fusion.86 = f32[1024,2,656]{0,2,1:T(8,128)} fusion(bf16[1024,2,656]{0,2,1:T(8,128)(2,1)} %all-gather.14.cloned.1.call-done, bf16[1024,1024]{1,0:T(8,128)(2,1)} %all-gather.12.cloned.1.call-done), kind=kOutput, calls=%fused_computation.71 | convolution fusion | flops 2751463424 | bytes 10158080 | tf_op jit(solution)/shard_map/dot_general | solution.py:15
  235.1 37.0 %all-gather.16.cloned.1.call-done = bf16[656,1024]{1,0:T(8,128)(2,1)} async-done(((bf16[656,128]{1,0:T(8,128)(2,1)}), bf16[656,1024]{1,0:T(8,128)(2,1)}) %all-gather.16.cloned.1.call-update) | async-done | bytes 1343504 | tf_op jit(solution)/shard_map/all_gather | solution.py:191
  272.1 22.9 %all-gather.18.cloned.1.call-done = bf16[1024,1024]{1,0:T(8,128)(2,1)} async-done(((bf16[256,1024]{1,0:T(8,128)(2,1)}), bf16[1024,1024]{1,0:T(8,128)(2,1)}) %all-gather.18.cloned.1.call-update) | async-done | bytes 2097168 | tf_op jit(solution)/shard_map/all_gather | solution.py:229
  295.0 7.5 %fusion.85 = (bf16[1024,656]{0,1:T(8,128)(2,1)S(1)}, bf16[1024,656]{0,1:T(8,128)(2,1)S(1)}, bf16[1024,656]{0,1:T(8,128)(2,1)}) fusion(f32[1024,2,656]{0,2,1:T(8,128)} %fusion.86, bf16[1024,1024]{1,0:T(8,128)(2,1)} %all-gather.18.cloned.1.call-done, bf16[656,1024]{1,0:T(8,128)(2,1)} %all-gather.16.cloned.1.call-done), kind=kOutput, calls=%fused_computation.67 | convolution fusion | flops 1386479616 | bytes 12845056 | tf_op jit(solution)/shard_map/dot_general | solution.py:25
  304.0 4.6 convolution_convert_fusion.1
  308.7 31.5 %reduce-scatter.21.cloned.1.call-done = bf16[256,1024]{1,0:T(8,128)(2,1)} async-done(((bf16[1024,1024]{1,0:T(8,128)(2,1)}), bf16[256,1024]{1,0:T(8,128)(2,1)}) %reduce-scatter.21.cloned.1.call-update) | async-done | bytes 524304 | tf_op jit(solution)/shard_map/reduce_scatter | solution.py:234
  341.9 2.4 fusion.124
  344.3 4.7 convolution_convert_fusion.5
  349.0 2.5 copy.38
  351.7 7.2 convolution_convert_fusion
  358.9 4.5 copy.42
  363.6 3.4 all-gather.20.cloned.1.call-done
  367.0 3.3 convolution_convert_fusion.6
  372.3 3.1 convolution_convert_fusion.7
  375.5 134.2 %while.28 = (s32[]{:T(128)}, f32[1024,4,64]{0,2,1:T(8,128)}, f32[1024,4,64]{0,2,1:T(8,128)}, f32[2,512,4,64]{1,0,3,2:T(2,128)}, s32[2]{0:T(128)S(1)}, /*index=5*...) while((s32[]{:T(128)}, f32[1024,4,64]{0,2,1:T(8,128)}, ...), condition=%wide.region_18.19_spmd.clone, body=%wide.region_16.18_spmd.clone.sunk | while | flops 1410865152 | bytes 123267416 | solution.py:163
  380.4 3.6 fusion.190
  384.1 4.5 fusion.187
  388.6 18.1 %fusion.191 = f32[1,512,4,64]{1,3,2,0:T(8,128)} fusion(bf16[1024,4,64]{0,2,1:T(8,128)(2,1)S(1)} %get-tuple-element.419, f32[4,512,1024]{2,1,0:T(8,128)} %fusion.187, f32[4,512,1024]{2,1,0:T(8,128)} %copy-done, f32[4,512]{1,0:T(4,128)S(1)} %dynamic-slice_bitcast_fusion.2, pred[512,1024]{1,0:T(8,128)(4,1)S(1)} %broadcast_compare_fusion.5), kind=kOutput, calls=%fused_computation.37.clone.1 | convolution fusion | flops 297798656 | bytes 18358272 | tf_op jit(solution)/shard_map/while/body/eval_jaxpr/hqk,khd->qhd/dot_general | solution.py:146
  406.6 23.1 %fusion.189 = f32[1024,4,64]{0,2,1:T(8,128)} fusion(f32[4,512,1024]{2,1,0:T(8,128)} %fusion.187, f32[4,512,1024]{2,1,0:T(8,128)} %copy-done, f32[4,512]{1,0:T(4,128)S(1)} %dynamic-slice_bitcast_fusion.2, pred[512,1024]{1,0:T(8,128)(4,1)S(1)} %broadcast_compare_fusion.5, f32[1024,4,64]{0,2,1:T(8,128)} %get-tuple-element.397, pred[]{:T(512)S(6)} %compare.3, ...), kind=kOutput, calls=%fused_computation.35.clone.1 | convolution fusion | flops 298322944 | bytes 36978692 | tf_op jit(solution)/shard_map/while/body/eval_jaxpr/hqk,qhd->khd/dot_general | solution.py:149
  431.4 10.3 %dynamic_update_slice.19 = f32[2,512,4,64]{1,0,3,2:T(2,128)} dynamic-update-slice(f32[2,512,4,64]{1,0,3,2:T(2,128)} %get-tuple-element.399, f32[1,512,4,64]{1,0,3,2:T(1,128)S(1)} %copy.59, s32[]{:T(128)S(6)} %copy.76, s32[]{:T(128)} %constant.35.clone.1..sunk.1, s32[]{:T(128)} %constant.35.clone.1..sunk.1, s32[]{:T(128)} %constant.35.clone.1..sunk.1) | dynamic-update-slice | bytes 1048580 | tf_op jit(solution)/shard_map/while/body/jit(dynamic_update_index_in_dim)/dynamic_update_slice | solution.py:123
  446.7 5.0 fusion.190
  451.7 4.5 fusion.187
  456.2 18.2 %fusion.191 = f32[1,512,4,64]{1,3,2,0:T(8,128)} fusion(bf16[1024,4,64]{0,2,1:T(8,128)(2,1)S(1)} %get-tuple-element.419, f32[4,512,1024]{2,1,0:T(8,128)} %fusion.187, f32[4,512,1024]{2,1,0:T(8,128)} %copy-done, f32[4,512]{1,0:T(4,128)S(1)} %dynamic-slice_bitcast_fusion.2, pred[512,1024]{1,0:T(8,128)(4,1)S(1)} %broadcast_compare_fusion.5), kind=kOutput, calls=%fused_computation.37.clone.1 | convolution fusion | flops 297798656 | bytes 18358272 | tf_op jit(solution)/shard_map/while/body/eval_jaxpr/hqk,khd->qhd/dot_general | solution.py:146
  474.4 23.2 %fusion.189 = f32[1024,4,64]{0,2,1:T(8,128)} fusion(f32[4,512,1024]{2,1,0:T(8,128)} %fusion.187, f32[4,512,1024]{2,1,0:T(8,128)} %copy-done, f32[4,512]{1,0:T(4,128)S(1)} %dynamic-slice_bitcast_fusion.2, pred[512,1024]{1,0:T(8,128)(4,1)S(1)} %broadcast_compare_fusion.5, f32[1024,4,64]{0,2,1:T(8,128)} %get-tuple-element.397, pred[]{:T(512)S(6)} %compare.3, ...), kind=kOutput, calls=%fused_computation.35.clone.1 | convolution fusion | flops 298322944 | bytes 36978692 | tf_op jit(solution)/shard_map/while/body/eval_jaxpr/hqk,qhd->khd/dot_general | solution.py:149
  499.2 10.3 %dynamic_update_slice.19 = f32[2,512,4,64]{1,0,3,2:T(2,128)} dynamic-update-slice(f32[2,512,4,64]{1,0,3,2:T(2,128)} %get-tuple-element.399, f32[1,512,4,64]{1,0,3,2:T(1,128)S(1)} %copy.59, s32[]{:T(128)S(6)} %copy.76, s32[]{:T(128)} %constant.35.clone.1..sunk.1, s32[]{:T(128)} %constant.35.clone.1..sunk.1, s32[]{:T(128)} %constant.35.clone.1..sunk.1) | dynamic-update-slice | bytes 1048580 | tf_op jit(solution)/shard_map/while/body/jit(dynamic_update_index_in_dim)/dynamic_update_slice | solution.py:123
  509.8 2.2 reshape.258
  515.5 3.0 fusion.94
  518.5 2.7 copy.40
  521.3 4.6 convolution_convert_fusion.3
  525.9 4.9 convolution_convert_fusion.4
  534.9 40.5 %reduce-scatter.27.cloned.1.call-done = bf16[128,256]{1,0:T(8,128)(2,1)} async-done(((bf16[1024,256]{1,0:T(8,128)(2,1)}), bf16[128,256]{1,0:T(8,128)(2,1)}) %reduce-scatter.27.cloned.1.call-update) | async-done | bytes 65552
  577.1 65.6 %reduce-scatter.25.cloned.1.call-done = bf16[128,768]{1,0:T(8,128)(2,1)} async-done(((bf16[1024,768]{1,0:T(8,128)(2,1)}), bf16[128,768]{1,0:T(8,128)(2,1)}) %reduce-scatter.25.cloned.1.call-update) | async-done | bytes 196624
  644.6 31.1 %reduce-scatter.23.cloned.1.call-done = bf16[256,1024]{1,0:T(8,128)(2,1)} async-done(((bf16[1024,1024]{1,0:T(8,128)(2,1)}), bf16[256,1024]{1,0:T(8,128)(2,1)}) %reduce-scatter.23.cloned.1.call-update) | async-done | bytes 524304 | tf_op jit(solution)/shard_map/reduce_scatter | solution.py:271
  677.2 39.4 %all-reduce = (f32[1024]{0:T(1024)}, f32[1024]{0:T(1024)}) all-reduce(f32[1024]{0:T(1024)S(1)} %get-tuple-element.153, f32[1024]{0:T(1024)S(1)} %get-tuple-element.151), channel_id=1, replica_groups=mesh['dp'=8,'tensor'=4] {'dp','tensor'}, use_global_device_ids=true, to_apply=%region_23.24 | all-reduce | flops 2048 | bytes 16384 | tf_op jit(solution)/shard_map/psum | solution.py:293
  716.7 3.0 fusion.111
  (171 shorter events, 50.4 us)
Async XLA Ops:
  7.2 6.2 copy-start.25
  7.2 6.5 copy-start.18
  7.2 54.6 %all-gather.10.cloned.1.call-start = ((), (), s32[]{:S(2)}) async-start(), calls=%async_computation.9 | async-start | bytes 1769472 | tf_op jit(solution)/shard_map/all_gather | solution.py:188
  7.9 76.8 %all-gather.8.cloned.1.call-start = ((), (), s32[]{:S(2)}) async-start(), calls=%async_computation.8 | async-start | bytes 2621440 | tf_op jit(solution)/shard_map/all_gather | solution.py:198
  9.2 1.4 copy-start.21
  13.2 131.5 %reduce-scatter.17.cloned.1.call-start = ((), (), s32[]{:S(2)}) async-start(), calls=%async_computation.10 | async-start | bytes 2621440 | tf_op jit(solution)/shard_map/reduce_scatter | solution.py:207
  44.4 65.9 %copy-start.7 = (bf16[256,1024]{1,0:T(8,128)(2,1)}, bf16[256,1024]{1,0:T(8,128)(2,1)S(1)}, u32[]{:S(2)}) copy-start(bf16[256,1024]{1,0:T(8,128)(2,1)S(1)} %all_gather.26) | copy-start | bytes 1572868
  44.9 44.1 %copy-start.12 = (f32[1024,32]{0,1:T(8,128)}, f32[1024,32]{0,1:T(8,128)S(1)}, u32[]{:S(2)}) copy-start(f32[1024,32]{0,1:T(8,128)S(1)} %get-tuple-element.220) | copy-start | bytes 393220
  44.9 44.1 %copy-start.14 = (f32[1024,32]{0,1:T(8,128)}, f32[1024,32]{0,1:T(8,128)S(1)}, u32[]{:S(2)}) copy-start(f32[1024,32]{0,1:T(8,128)S(1)} %get-tuple-element.221) | copy-start | bytes 393220
  92.8 2.3 copy-start.16
  98.2 0.8 copy-start.17
  102.4 2.3 copy-start.16
  107.8 0.8 copy-start.17
  110.2 0.8 copy-start.9
  111.0 33.7 %copy-start.1 = (bf16[256,1024]{1,0:T(8,128)(2,1)S(1)}, bf16[256,1024]{1,0:T(8,128)(2,1)}, u32[]{:S(2)}) copy-start(bf16[256,1024]{1,0:T(8,128)(2,1)} %param.13) | copy-start | bytes 1572868
  113.1 34.2 %copy-start.19 = (f32[1024]{0:T(1024)S(1)}, f32[1024]{0:T(1024)}, u32[]{:S(2)}) copy-start(f32[1024]{0:T(1024)} %param.17) | copy-start | bytes 12292
  113.1 91.3 %all-gather.14.cloned.1.call-start = ((), (), s32[]{:S(2)}) async-start(), calls=%async_computation.12 | async-start | bytes 3022848 | tf_op jit(solution)/shard_map/all_gather | solution.py:190
  113.7 113.6 %all-gather.12.cloned.1.call-start = ((), (), s32[]{:S(2)}) async-start(), calls=%async_computation.11 | async-start | bytes 2621440 | tf_op jit(solution)/shard_map/all_gather | solution.py:215
  149.4 122.6 %all-gather.16.cloned.1.call-start = ((), (), s32[]{:S(2)}) async-start(), calls=%async_computation.13 | async-start | bytes 1511424 | tf_op jit(solution)/shard_map/all_gather | solution.py:191
  150.0 145.0 %all-gather.18.cloned.1.call-start = ((), (), s32[]{:S(2)}) async-start(), calls=%async_computation.15 | async-start | bytes 2621440 | tf_op jit(solution)/shard_map/all_gather | solution.py:229
  150.8 189.5 %reduce-scatter.21.cloned.1.call-start = ((), (), s32[]{:S(2)}) async-start(), calls=%async_computation.16 | async-start | bytes 2621440 | tf_op jit(solution)/shard_map/reduce_scatter | solution.py:234
  295.0 9.0 %copy-start.26 = (bf16[1024,2,656]{0,2,1:T(8,128)(2,1)S(1)}, bf16[1024,2,656]{0,2,1:T(8,128)(2,1)}, u32[]{:S(2)}) copy-start(bf16[1024,2,656]{0,2,1:T(8,128)(2,1)} %all-gather.14.cloned.1.call-done) | copy-start | bytes 8060932
  302.5 1.1 copy-start.28
  302.5 1.5 copy-start.29
  304.0 36.3 %copy-start.2 = (bf16[256,1024]{1,0:T(8,128)(2,1)S(1)}, bf16[256,1024]{1,0:T(8,128)(2,1)}, u32[]{:S(2)}) copy-start(bf16[256,1024]{1,0:T(8,128)(2,1)} %reduce-scatter.17.cloned.1.call-done) | copy-start | bytes 1572868
  308.6 33.3 %copy-start.4 = (bf16[256,1024]{1,0:T(8,128)(2,1)S(1)}, bf16[256,1024]{1,0:T(8,128)(2,1)}, u32[]{:S(2)}) copy-start(bf16[256,1024]{1,0:T(8,128)(2,1)} %param.21) | copy-start | bytes 1572868
  308.6 58.4 %all-gather.20.cloned.1.call-start = ((), (), s32[]{:S(2)}) async-start(), calls=%async_computation.17 | async-start | bytes 2621440 | tf_op jit(solution)/shard_map/all_gather | solution.py:244
  344.3 186.6 %reduce-scatter.31.cloned.1.call-start = ((), (), s32[]{:S(2)}) async-start(), calls=%async_computation.22 | async-start | bytes 1769472
  351.6 181.2 %reduce-scatter.29.cloned.1.call-start = ((), (), s32[]{:S(2)}) async-start(), calls=%async_computation.21 | async-start | bytes 3244032
  363.4 8.9 %copy-start.8 = (bf16[256,1024]{1,0:T(8,128)(2,1)S(1)}, bf16[256,1024]{1,0:T(8,128)(2,1)}, u32[]{:S(2)}) copy-start(bf16[256,1024]{1,0:T(8,128)(2,1)} %copy-done.7) | copy-start | bytes 1572868
  363.4 212.0 %reduce-scatter.27.cloned.1.call-start = ((), (), s32[]{:S(2)}) async-start(), calls=%async_computation.20 | async-start | bytes 589824
  379.1 1.3 copy-start.6
  380.4 3.6 copy-start
  445.3 1.3 copy-start.6
  446.7 5.0 copy-start
  509.7 2.3 copy-start.13
  509.7 2.3 copy-start.15
  511.9 130.8 %reduce-scatter.25.cloned.1.call-start = ((), (), s32[]{:S(2)}) async-start(), calls=%async_computation.19 | async-start | bytes 1769472
  513.6 1.9 copy-start.27
  515.3 3.2 copy-start.10
  518.5 2.8 copy-start.11
  521.2 154.4 %reduce-scatter.23.cloned.1.call-start = ((), (), s32[]{:S(2)}) async-start(), calls=%async_computation.18 | async-start | bytes 2621440 | tf_op jit(solution)/shard_map/reduce_scatter | solution.py:271
  525.9 190.8 %reduce-scatter.19.cloned.1.call-start = ((), (), s32[]{:S(2)}) async-start(), calls=%async_computation.14 | async-start | bytes 2621440 | tf_op jit(solution)/shard_map/reduce_scatter | solution.py:222
  530.8 144.8 %copy-start.20 = (f32[1024]{0:T(1024)S(1)}, f32[1024]{0:T(1024)}, u32[]{:S(2)}) copy-start(f32[1024]{0:T(1024)} %param.14) | copy-start | bytes 12292
  530.8 144.8 %copy-start.22 = (f32[256]{0:T(256)S(1)}, f32[256]{0:T(256)}, u32[]{:S(2)}) copy-start(f32[256]{0:T(256)} %copy-done.21) | copy-start | bytes 3076
  530.8 144.8 %copy-start.24 = (f32[256]{0:T(256)S(1)}, f32[256]{0:T(256)}, u32[]{:S(2)}) copy-start(f32[256]{0:T(256)} %copy-done.23) | copy-start | bytes 3076
  530.9 185.8 %copy-start.3 = (bf16[256,1024]{1,0:T(8,128)(2,1)S(1)}, bf16[256,1024]{1,0:T(8,128)(2,1)}, u32[]{:S(2)}) copy-start(bf16[256,1024]{1,0:T(8,128)(2,1)} %reduce-scatter.21.cloned.1.call-done) | copy-start | bytes 1572868
  530.9 185.8 %copy-start.5 = (bf16[256,1024]{1,0:T(8,128)(2,1)S(1)}, bf16[256,1024]{1,0:T(8,128)(2,1)}, u32[]{:S(2)}) copy-start(bf16[256,1024]{1,0:T(8,128)(2,1)} %param.21) | copy-start | bytes 1572868
  (1 other events, 0.6 us)
Sparse Core Ops, SparseCore 0:
  10.1 51.6 all-gather.9
  63.9 20.7 all-gather.7
  113.2 31.4 reduce-scatter.16
  146.8 57.6 all-gather.13
  206.5 20.7 all-gather.11
  229.4 42.5 all-gather.15
  273.7 21.2 all-gather.17
  308.7 31.4 reduce-scatter.20
  344.4 22.5 all-gather.19
  370.3 64.9 reduce-scatter.30
  439.3 70.6 reduce-scatter.28
  514.1 61.2 reduce-scatter.26
  578.9 63.7 reduce-scatter.24
  645.2 30.3 reduce-scatter.22
  678.0 31.4 reduce-scatter.18
where the time goes:
time: 736 us; the launch traced here: 726 us
  waiting for transfers between devices  382 us (52%)
  matrix products  169 us (23%)
  blocking collectives  70.2 us (10%)
  local copies, waits for them, and re-layouts  51.6 us (7%)
  other arithmetic  31.6 us (4%)
  between operations  14.6 us (2%)
    unnamed x19, waiting for transfers between devices  109 us
    all_gather x1, waiting for transfers between devices, body(): lax.all_gather(in_weight, 'dp', axis=0, tiled=True)  53.2 us
    dot_general x2, matrix products, block_step(): jnp.einsum('hqk,qhd->khd', grad_scores, query_part, preferred_element_typ...  46.3 us
    psum x1, blocking collectives, body(): lax.psum((attn_gain_part, mlp_gain_part), ('dp', 'tensor'))  39.4 us
    all_gather x1, waiting for transfers between devices, body(): lax.all_gather(down_weight, 'dp', axis=1, tiled=True)  37 us
    dot_general x2, matrix products, block_step(): jnp.einsum('hqk,khd->qhd', grad_scores, key_rows, preferred_element_type=...  36.2 us
    reduce_scatter x1, waiting for transfers between devices, body(): lax.psum_scatter(dot_last(grad_lifted, in_flat).astype(jnp.bfloat16), 'te...  31.5 us
    reduce_scatter x1, waiting for transfers between devices, body(): lax.psum_scatter(dot_last(grad_mixed, qkv_flat).astype(jnp.bfloat16), 'te...  31.1 us
  transfers between devices with their start and end apart: 15, of which 12 were waited for; matrix products, arithmetic and copies ran while one was open for 28% of the time, Pallas kernels for 0%

commit v1 on v0

--- a/solution.py
+++ b/solution.py
@@ -212,7 +212,14 @@
     ).astype(jnp.float32)
     normed_mlp, unit_mlp, inverse_mlp = layer_norm(residual, mlp_gain)
     mlp_input = normed_mlp.astype(jnp.bfloat16)
-    mlp_rows = lax.all_gather(mlp_input, "tensor", axis=0, tiled=True)
+    ring = [mlp_input]
+    for hop in range(3):
+        ring.append(lax.ppermute(ring[-1], "tensor", [(dev, (dev + 1) % 4) for dev in range(4)]))
+    mlp_rows = jnp.roll(
+        jnp.concatenate(ring[::-1], axis=0),
+        (lax.axis_index("tensor") + 1) * ring[0].shape[0],
+        axis=0,
+    )
     in_flat = in_full.reshape(model_width, -1)
     lifted = dot_plain(mlp_rows, in_flat).reshape(pack_rows, 2, hidden_local)
     act_gelu, act_slope = gelu_parts(lifted[:, 0])

time: 736 us -> 713 us (0.969)
  waiting for transfers between devices: 382 us -> 345 us
  local copies, waits for them, and re-layouts: 51.6 us -> 62.6 us
    all_gather x1, waiting for transfers between devices: 53.2 us -> 18.1 us  [body(): lax.all_gather(in_weight, 'dp', axis=0, tiled=True)]
    ppermute x0 -> x3, waiting for transfers between devices: none -> 26.1 us  [body(): lax.ppermute(ring[-1], 'tensor', [(dev, (dev + 1) % 4) for dev in range(4)])]
    all_gather x1 -> x0, waiting for transfers between devices: 22.9 us -> none  [body(): mlp_rows = lax.all_gather(mlp_input, 'tensor', axis=0, tiled=True)]
    unnamed x61 -> x64, local copies, waits for them, and re-layouts: 19.4 us -> 29.5 us
    unnamed x19 -> x18, waiting for transfers between devices: 109 us -> 108 us
  transfers between devices with their start and end apart: 15 -> 17, of which waited for: 12 -> 14; matrix products, arithmetic and copies ran while one was open for 28% -> 31% of each run, Pallas kernels for 0% -> 0%
where the time goes in v1:
time: 713 us; the launch traced here: 702 us
  waiting for transfers between devices  345 us (48%)
  matrix products  169 us (24%)
  blocking collectives  71 us (10%)
  local copies, waits for them, and re-layouts  62.6 us (9%)
  other arithmetic  32.1 us (5%)
  between operations  14.6 us (2%)
    unnamed x18, waiting for transfers between devices  108 us
    dot_general x2, matrix products, block_step(): jnp.einsum('hqk,qhd->khd', grad_scores, query_part, preferred_element_typ...  46.3 us
    psum x1, blocking collectives, body(): lax.psum((attn_gain_part, mlp_gain_part), ('dp', 'tensor'))  39.4 us
    dot_general x2, matrix products, block_step(): jnp.einsum('hqk,khd->qhd', grad_scores, key_rows, preferred_element_type=...  36.3 us
    all_gather x1, waiting for transfers between devices, body(): lax.all_gather(down_weight, 'dp', axis=1, tiled=True)  35.2 us
    all_gather x1, blocking collectives, body(): lax.all_gather(out_weight, 'dp', axis=1, tiled=True)  31.6 us
    reduce_scatter x1, waiting for transfers between devices, body(): lax.psum_scatter(dot_last(grad_lifted, in_flat).astype(jnp.bfloat16), 'te...  31.5 us
    reduce_scatter x1, waiting for transfers between devices, body(): lax.psum_scatter(dot_last(grad_mixed, qkv_flat).astype(jnp.bfloat16), 'te...  31.2 us
  transfers between devices with their start and end apart: 17, of which 14 were waited for; matrix products, arithmetic and copies ran while one was open for 31% of the time, Pallas kernels for 0%

profile of v1, /device:TPU:0, one launch (start us, length us, event | category | flops | bytes accessed | tf_op | source)
XLA Modules:
  0.0 702.3 jit_solution(13707431006040212838)
XLA Ops:
  14.9 31.6 %all_gather.23 = bf16[256,1024]{1,0:T(8,128)(2,1)S(1)} all-gather(bf16[256,128]{1,0:T(8,128)(2,1)} %param.16), channel_id=1, replica_groups=mesh['dp'=8,'tensor'=4] {'dp'}, dimensions={1}, use_global_device_ids=true | all-gather | bytes 589824 | tf_op jit(solution)/shard_map/all_gather | solution.py:189
  47.1 14.4 %all-gather.9.cloned.1.call-done = bf16[1024,4,192]{0,2,1:T(8,128)(2,1)} async-done(((bf16[128,4,192]{0,2,1:T(8,128)(2,1)}), bf16[1024,4,192]{0,2,1:T(8,128)(2,1)}) %all-gather.9.cloned.1.call-update) | async-done | bytes 1572880 | tf_op jit(solution)/shard_map/all_gather | solution.py:188
  61.5 23.4 %all-gather.7.cloned.1.call-done = bf16[1024,1024]{1,0:T(8,128)(2,1)} async-done(((bf16[256,1024]{1,0:T(8,128)(2,1)}), bf16[1024,1024]{1,0:T(8,128)(2,1)}) %all-gather.7.cloned.1.call-update) | async-done | bytes 2097168 | tf_op jit(solution)/shard_map/all_gather | solution.py:198
  84.9 3.9 fusion.89
  89.5 19.1 %while.27 = (s32[]{:T(128)}, bf16[2,512,4,64]{1,3,2,0:T(8,128)(2,1)}, f32[2,4,512]{2,1,0:T(4,128)S(1)}, s32[2]{0:T(128)S(1)}, s32[1024]{0:T(1024)S(1)}, /*index=...) while((s32[]{:T(128)}, ...), condition=%wide.region_8.9_spmd, body=%wide.region_5.8_spmd.sunk | while | flops 562558976 | bytes 33368320 | solution.py:123
  92.9 2.3 fusion.176
  95.3 3.0 fusion.177
  102.5 2.3 fusion.176
  104.8 3.0 fusion.177
  114.5 30.4 %reduce-scatter.17.cloned.1.call-done = bf16[256,1024]{1,0:T(8,128)(2,1)} async-done(((bf16[1024,1024]{1,0:T(8,128)(2,1)}), bf16[256,1024]{1,0:T(8,128)(2,1)}) %reduce-scatter.17.cloned.1.call-update) | async-done | bytes 524304 | tf_op jit(solution)/shard_map/reduce_scatter | solution.py:207
  148.9 8.5 %collective-permute-done = bf16[256,1024]{1,0:T(8,128)(2,1)S(1)} collective-permute-done((bf16[256,1024]{1,0:T(8,128)(2,1)S(1)}, bf16[256,1024]{1,0:T(8,128)(2,1)S(1)}, u32[]{:S(2)}, u32[]{:S(2)}) %collective-permute-start) | collective-permute-done | bytes 524320 | tf_op jit(solution)/shard_map/ppermute | solution.py:217
  157.5 8.7 %collective-permute-done.1 = bf16[256,1024]{1,0:T(8,128)(2,1)} collective-permute-done((bf16[256,1024]{1,0:T(8,128)(2,1)S(1)}, bf16[256,1024]{1,0:T(8,128)(2,1)}, u32[]{:S(2)}, u32[]{:S(2)}) %collective-permute-start.1) | collective-permute-done | bytes 524320 | tf_op jit(solution)/shard_map/ppermute | solution.py:217
  166.6 8.9 %collective-permute-done.2 = bf16[256,1024]{1,0:T(8,128)(2,1)} collective-permute-done((bf16[256,1024]{1,0:T(8,128)(2,1)}, bf16[256,1024]{1,0:T(8,128)(2,1)}, u32[]{:S(2)}, u32[]{:S(2)}) %collective-permute-start.2) | collective-permute-done | bytes 524320 | tf_op jit(solution)/shard_map/ppermute | solution.py:217
  186.5 18.1 %all-gather.11.cloned.1.call-done = bf16[1024,2,656]{0,2,1:T(8,128)(2,1)} async-done(((bf16[128,2,656]{0,2,1:T(8,128)(2,1)}), bf16[1024,2,656]{0,2,1:T(8,128)(2,1)}) %all-gather.11.cloned.1.call-update) | async-done | bytes 2686992 | tf_op jit(solution)/shard_map/all_gather | solution.py:190
  204.7 7.7 %fusion.86 = f32[1024,2,656]{0,2,1:T(8,128)} fusion(bf16[1024,2,656]{0,2,1:T(8,128)(2,1)} %all-gather.11.cloned.1.call-done, bf16[2048,1024]{1,0:T(8,128)(2,1)} %constant_dynamic-update-slice_fusion, s32[]{:T(128)S(6)} %select_n.38), kind=kOutput, calls=%fused_computation.71 | convolution fusion | flops 2751463424 | bytes 10158084 | tf_op jit(solution)/shard_map/dot_general | solution.py:15
  212.4 35.2 %all-gather.13.cloned.1.call-done = bf16[656,1024]{1,0:T(8,128)(2,1)} async-done(((bf16[656,128]{1,0:T(8,128)(2,1)}), bf16[656,1024]{1,0:T(8,128)(2,1)}) %all-gather.13.cloned.1.call-update) | async-done | bytes 1343504 | tf_op jit(solution)/shard_map/all_gather | solution.py:191
  247.6 22.7 %all-gather.15.cloned.1.call-done = bf16[1024,1024]{1,0:T(8,128)(2,1)} async-done(((bf16[256,1024]{1,0:T(8,128)(2,1)}), bf16[1024,1024]{1,0:T(8,128)(2,1)}) %all-gather.15.cloned.1.call-update) | async-done | bytes 2097168 | tf_op jit(solution)/shard_map/all_gather | solution.py:236
  270.3 7.5 %fusion.85 = (bf16[1024,656]{0,1:T(8,128)(2,1)S(1)}, bf16[1024,656]{0,1:T(8,128)(2,1)S(1)}, bf16[1024,656]{0,1:T(8,128)(2,1)}) fusion(f32[1024,2,656]{0,2,1:T(8,128)} %fusion.86, bf16[1024,1024]{1,0:T(8,128)(2,1)} %all-gather.15.cloned.1.call-done, bf16[656,1024]{1,0:T(8,128)(2,1)} %all-gather.13.cloned.1.call-done), kind=kOutput, calls=%fused_computation.67 | convolution fusion | flops 1386479616 | bytes 12845056 | tf_op jit(solution)/shard_map/dot_general | solution.py:25
  279.3 4.7 convolution_convert_fusion.1
  284.0 31.5 %reduce-scatter.21.cloned.1.call-done = bf16[256,1024]{1,0:T(8,128)(2,1)} async-done(((bf16[1024,1024]{1,0:T(8,128)(2,1)}), bf16[256,1024]{1,0:T(8,128)(2,1)}) %reduce-scatter.21.cloned.1.call-update) | async-done | bytes 524304 | tf_op jit(solution)/shard_map/reduce_scatter | solution.py:241
  317.2 2.4 fusion.128
  319.7 4.7 convolution_convert_fusion.5
  324.4 2.5 copy.38
  327.0 7.2 %convolution_convert_fusion = bf16[1024,1312]{0,1:T(8,128)(2,1)} fusion(bf16[2048,1024]{1,0:T(8,128)(2,1)} %constant_dynamic-update-slice_fusion, s32[]{:T(128)S(6)} %select_n.38, bf16[1024,656]{0,1:T(8,128)(2,1)} %copy-done.27, bf16[1024,656]{0,1:T(8,128)(2,1)} %copy-done.26), kind=kOutput, calls=%fused_computation.61 | convolution fusion | flops 2758180864 | bytes 7471108 | tf_op jit(solution)/shard_map/dot_general | solution.py:19
  334.2 4.5 copy.42
  338.8 3.6 all-gather.17.cloned.1.call-done
  342.4 3.3 convolution_convert_fusion.6
  347.7 3.1 convolution_convert_fusion.7
  350.8 134.4 %while.28 = (s32[]{:T(128)}, f32[1024,4,64]{0,2,1:T(8,128)}, f32[1024,4,64]{0,2,1:T(8,128)}, f32[2,512,4,64]{1,0,3,2:T(2,128)}, s32[2]{0:T(128)S(1)}, /*index=5*...) while((s32[]{:T(128)}, f32[1024,4,64]{0,2,1:T(8,128)}, ...), condition=%wide.region_18.19_spmd.clone, body=%wide.region_16.18_spmd.clone.sunk | while | flops 1410865152 | bytes 123267416 | solution.py:163
  356.0 3.6 fusion.193
  359.6 4.5 fusion.190
  364.1 18.1 %fusion.194 = f32[1,512,4,64]{1,3,2,0:T(8,128)} fusion(bf16[1024,4,64]{0,2,1:T(8,128)(2,1)S(1)} %get-tuple-element.419, f32[4,512,1024]{2,1,0:T(8,128)} %fusion.190, f32[4,512,1024]{2,1,0:T(8,128)} %copy-done, f32[4,512]{1,0:T(4,128)S(1)} %dynamic-slice_bitcast_fusion.2, pred[512,1024]{1,0:T(8,128)(4,1)S(1)} %broadcast_compare_fusion.5), kind=kOutput, calls=%fused_computation.37.clone.1 | convolution fusion | flops 297798656 | bytes 18358272 | tf_op jit(solution)/shard_map/while/body/eval_jaxpr/hqk,khd->qhd/dot_general | solution.py:146
  382.2 23.1 %fusion.192 = f32[1024,4,64]{0,2,1:T(8,128)} fusion(f32[4,512,1024]{2,1,0:T(8,128)} %fusion.190, f32[4,512,1024]{2,1,0:T(8,128)} %copy-done, f32[4,512]{1,0:T(4,128)S(1)} %dynamic-slice_bitcast_fusion.2, pred[512,1024]{1,0:T(8,128)(4,1)S(1)} %broadcast_compare_fusion.5, f32[1024,4,64]{0,2,1:T(8,128)} %get-tuple-element.397, pred[]{:T(512)S(6)} %compare.4, ...), kind=kOutput, calls=%fused_computation.35.clone.1 | convolution fusion | flops 298322944 | bytes 36978692 | tf_op jit(solution)/shard_map/while/body/eval_jaxpr/hqk,qhd->khd/dot_general | solution.py:149
  406.9 10.3 %dynamic_update_slice.19 = f32[2,512,4,64]{1,0,3,2:T(2,128)} dynamic-update-slice(f32[2,512,4,64]{1,0,3,2:T(2,128)} %get-tuple-element.399, f32[1,512,4,64]{1,0,3,2:T(1,128)S(1)} %copy.59, s32[]{:T(128)S(6)} %copy.83, s32[]{:T(128)} %constant.91.clone.1..sunk.1, s32[]{:T(128)} %constant.91.clone.1..sunk.1, s32[]{:T(128)} %constant.91.clone.1..sunk.1) | dynamic-update-slice | bytes 1048580 | tf_op jit(solution)/shard_map/while/body/jit(dynamic_update_index_in_dim)/dynamic_update_slice | solution.py:123
  422.2 5.0 fusion.193
  427.2 4.5 fusion.190
  431.7 18.2 %fusion.194 = f32[1,512,4,64]{1,3,2,0:T(8,128)} fusion(bf16[1024,4,64]{0,2,1:T(8,128)(2,1)S(1)} %get-tuple-element.419, f32[4,512,1024]{2,1,0:T(8,128)} %fusion.190, f32[4,512,1024]{2,1,0:T(8,128)} %copy-done, f32[4,512]{1,0:T(4,128)S(1)} %dynamic-slice_bitcast_fusion.2, pred[512,1024]{1,0:T(8,128)(4,1)S(1)} %broadcast_compare_fusion.5), kind=kOutput, calls=%fused_computation.37.clone.1 | convolution fusion | flops 297798656 | bytes 18358272 | tf_op jit(solution)/shard_map/while/body/eval_jaxpr/hqk,khd->qhd/dot_general | solution.py:146
  449.9 23.2 %fusion.192 = f32[1024,4,64]{0,2,1:T(8,128)} fusion(f32[4,512,1024]{2,1,0:T(8,128)} %fusion.190, f32[4,512,1024]{2,1,0:T(8,128)} %copy-done, f32[4,512]{1,0:T(4,128)S(1)} %dynamic-slice_bitcast_fusion.2, pred[512,1024]{1,0:T(8,128)(4,1)S(1)} %broadcast_compare_fusion.5, f32[1024,4,64]{0,2,1:T(8,128)} %get-tuple-element.397, pred[]{:T(512)S(6)} %compare.4, ...), kind=kOutput, calls=%fused_computation.35.clone.1 | convolution fusion | flops 298322944 | bytes 36978692 | tf_op jit(solution)/shard_map/while/body/eval_jaxpr/hqk,qhd->khd/dot_general | solution.py:149
  474.7 10.3 %dynamic_update_slice.19 = f32[2,512,4,64]{1,0,3,2:T(2,128)} dynamic-update-slice(f32[2,512,4,64]{1,0,3,2:T(2,128)} %get-tuple-element.399, f32[1,512,4,64]{1,0,3,2:T(1,128)S(1)} %copy.59, s32[]{:T(128)S(6)} %copy.83, s32[]{:T(128)} %constant.91.clone.1..sunk.1, s32[]{:T(128)} %constant.91.clone.1..sunk.1, s32[]{:T(128)} %constant.91.clone.1..sunk.1) | dynamic-update-slice | bytes 1048580 | tf_op jit(solution)/shard_map/while/body/jit(dynamic_update_index_in_dim)/dynamic_update_slice | solution.py:123
  491.0 3.0 fusion.96
  493.9 2.7 copy.40
  496.7 4.6 convolution_convert_fusion.3
  501.4 4.9 convolution_convert_fusion.4
  510.4 40.8 %reduce-scatter.27.cloned.1.call-done = bf16[128,256]{1,0:T(8,128)(2,1)} async-done(((bf16[1024,256]{1,0:T(8,128)(2,1)}), bf16[128,256]{1,0:T(8,128)(2,1)}) %reduce-scatter.27.cloned.1.call-update) | async-done | bytes 65552
  552.9 65.6 %reduce-scatter.25.cloned.1.call-done = bf16[128,768]{1,0:T(8,128)(2,1)} async-done(((bf16[1024,768]{1,0:T(8,128)(2,1)}), bf16[128,768]{1,0:T(8,128)(2,1)}) %reduce-scatter.25.cloned.1.call-update) | async-done | bytes 196624
  620.3 31.2 %reduce-scatter.23.cloned.1.call-done = bf16[256,1024]{1,0:T(8,128)(2,1)} async-done(((bf16[1024,1024]{1,0:T(8,128)(2,1)}), bf16[256,1024]{1,0:T(8,128)(2,1)}) %reduce-scatter.23.cloned.1.call-update) | async-done | bytes 524304 | tf_op jit(solution)/shard_map/reduce_scatter | solution.py:278
  653.1 39.4 %all-reduce = (f32[1024]{0:T(1024)}, f32[1024]{0:T(1024)}) all-reduce(f32[1024]{0:T(1024)S(1)} %get-tuple-element.153, f32[1024]{0:T(1024)S(1)} %get-tuple-element.151), channel_id=1, replica_groups=mesh['dp'=8,'tensor'=4] {'dp','tensor'}, use_global_device_ids=true, to_apply=%region_23.24 | all-reduce | flops 2048 | bytes 16384 | tf_op jit(solution)/shard_map/psum | solution.py:300
  692.6 3.0 fusion.113
  (178 shorter events, 65.3 us)
Async XLA Ops:
  7.2 54.3 %all-gather.9.cloned.1.call-start = ((), (), s32[]{:S(2)}) async-start(), calls=%async_computation.9 | async-start | bytes 1769472 | tf_op jit(solution)/shard_map/all_gather | solution.py:188
  7.9 77.0 %all-gather.7.cloned.1.call-start = ((), (), s32[]{:S(2)}) async-start(), calls=%async_computation.8 | async-start | bytes 2621440 | tf_op jit(solution)/shard_map/all_gather | solution.py:198
  9.1 1.4 copy-start.20
  13.2 131.7 %reduce-scatter.17.cloned.1.call-start = ((), (), s32[]{:S(2)}) async-start(), calls=%async_computation.10 | async-start | bytes 2621440 | tf_op jit(solution)/shard_map/reduce_scatter | solution.py:207
  46.5 63.9 %copy-start.7 = (bf16[256,1024]{1,0:T(8,128)(2,1)}, bf16[256,1024]{1,0:T(8,128)(2,1)S(1)}, u32[]{:S(2)}) copy-start(bf16[256,1024]{1,0:T(8,128)(2,1)S(1)} %all_gather.23) | copy-start | bytes 1572868
  47.0 42.0 %copy-start.12 = (f32[1024,32]{0,1:T(8,128)}, f32[1024,32]{0,1:T(8,128)S(1)}, u32[]{:S(2)}) copy-start(f32[1024,32]{0,1:T(8,128)S(1)} %get-tuple-element.220) | copy-start | bytes 393220
  47.1 42.0 %copy-start.14 = (f32[1024,32]{0,1:T(8,128)}, f32[1024,32]{0,1:T(8,128)S(1)}, u32[]{:S(2)}) copy-start(f32[1024,32]{0,1:T(8,128)S(1)} %get-tuple-element.221) | copy-start | bytes 393220
  92.9 2.3 copy-start.16
  98.3 0.8 copy-start.17
  102.5 2.3 copy-start.16
  107.8 0.8 copy-start.17
  108.6 36.3 %copy-start.1 = (bf16[256,1024]{1,0:T(8,128)(2,1)S(1)}, bf16[256,1024]{1,0:T(8,128)(2,1)}, u32[]{:S(2)}) copy-start(bf16[256,1024]{1,0:T(8,128)(2,1)} %param.13) | copy-start | bytes 1572868
  110.3 37.2 %copy-start.18 = (f32[1024]{0:T(1024)S(1)}, f32[1024]{0:T(1024)}, u32[]{:S(2)}) copy-start(f32[1024]{0:T(1024)} %param.17) | copy-start | bytes 12292
  110.4 0.8 copy-start.9
  113.3 91.4 %all-gather.11.cloned.1.call-start = ((), (), s32[]{:S(2)}) async-start(), calls=%async_computation.11 | async-start | bytes 3022848 | tf_op jit(solution)/shard_map/all_gather | solution.py:190
  113.9 133.7 %all-gather.13.cloned.1.call-start = ((), (), s32[]{:S(2)}) async-start(), calls=%async_computation.12 | async-start | bytes 1511424 | tf_op jit(solution)/shard_map/all_gather | solution.py:191
  114.5 155.8 %all-gather.15.cloned.1.call-start = ((), (), s32[]{:S(2)}) async-start(), calls=%async_computation.14 | async-start | bytes 2621440 | tf_op jit(solution)/shard_map/all_gather | solution.py:236
  148.8 8.7 %collective-permute-start = (bf16[256,1024]{1,0:T(8,128)(2,1)S(1)}, bf16[256,1024]{1,0:T(8,128)(2,1)S(1)}, u32[]{:S(2)}, u32[]{:S(2)}) collective-permute-start(bf16[256,1024]{1,0:T(8,128)(2,1)S(1)} %multiply_convert_fusion.3), channel_id=1, source_target_pairs={{0,1},{1,2},{2,3},{3,0},{4,5},{5,6},{6,7},{7,4},{8,9},{9,10},{10,1... | collective-permute-start | bytes 1572872 | tf_op jit(solution)/shard_map/ppermute | solution.py:217
  148.9 166.7 %reduce-scatter.21.cloned.1.call-start = ((), (), s32[]{:S(2)}) async-start(), calls=%async_computation.15 | async-start | bytes 2621440 | tf_op jit(solution)/shard_map/reduce_scatter | solution.py:241
  157.5 8.7 %collective-permute-start.1 = (bf16[256,1024]{1,0:T(8,128)(2,1)S(1)}, bf16[256,1024]{1,0:T(8,128)(2,1)}, u32[]{:S(2)}, u32[]{:S(2)}) collective-permute-start(bf16[256,1024]{1,0:T(8,128)(2,1)S(1)} %collective-permute-done), channel_id=1, source_target_pairs={{0,1},{1,2},{2,3},{3,0},{4,5},{5,6},{6,7},{7,4},{8,9},{9,10},{10,1... | collective-permute-start | bytes 1572872 | tf_op jit(solution)/shard_map/ppermute | solution.py:217
  166.2 9.4 %collective-permute-start.2 = (bf16[256,1024]{1,0:T(8,128)(2,1)}, bf16[256,1024]{1,0:T(8,128)(2,1)}, u32[]{:S(2)}, u32[]{:S(2)}) collective-permute-start(bf16[256,1024]{1,0:T(8,128)(2,1)} %collective-permute-done.1), channel_id=1, source_target_pairs={{0,1},{1,2},{2,3},{3,0},{4,5},{5,6},{6,7},{7,4},{8,9},{9,10},{10,1... | collective-permute-start | bytes 1572872 | tf_op jit(solution)/shard_map/ppermute | solution.py:217
  270.3 9.0 %copy-start.24 = (bf16[1024,2,656]{0,2,1:T(8,128)(2,1)S(1)}, bf16[1024,2,656]{0,2,1:T(8,128)(2,1)}, u32[]{:S(2)}) copy-start(bf16[1024,2,656]{0,2,1:T(8,128)(2,1)} %all-gather.11.cloned.1.call-done) | copy-start | bytes 8060932
  277.8 1.1 copy-start.26
  277.8 1.5 copy-start.27
  279.3 36.3 %copy-start.2 = (bf16[256,1024]{1,0:T(8,128)(2,1)S(1)}, bf16[256,1024]{1,0:T(8,128)(2,1)}, u32[]{:S(2)}) copy-start(bf16[256,1024]{1,0:T(8,128)(2,1)} %reduce-scatter.17.cloned.1.call-done) | copy-start | bytes 1572868
  279.3 37.9 %copy-start.4 = (bf16[256,1024]{1,0:T(8,128)(2,1)S(1)}, bf16[256,1024]{1,0:T(8,128)(2,1)}, u32[]{:S(2)}) copy-start(bf16[256,1024]{1,0:T(8,128)(2,1)} %param.21) | copy-start | bytes 1572868
  284.0 58.4 %all-gather.17.cloned.1.call-start = ((), (), s32[]{:S(2)}) async-start(), calls=%async_computation.16 | async-start | bytes 2621440 | tf_op jit(solution)/shard_map/all_gather | solution.py:251
  319.6 186.7 %reduce-scatter.31.cloned.1.call-start = ((), (), s32[]{:S(2)}) async-start(), calls=%async_computation.21 | async-start | bytes 1769472
  326.9 181.4 %reduce-scatter.29.cloned.1.call-start = ((), (), s32[]{:S(2)}) async-start(), calls=%async_computation.20 | async-start | bytes 3244032
  338.7 9.0 %copy-start.8 = (bf16[256,1024]{1,0:T(8,128)(2,1)S(1)}, bf16[256,1024]{1,0:T(8,128)(2,1)}, u32[]{:S(2)}) copy-start(bf16[256,1024]{1,0:T(8,128)(2,1)} %copy-done.7) | copy-start | bytes 1572868
  338.8 212.5 %reduce-scatter.27.cloned.1.call-start = ((), (), s32[]{:S(2)}) async-start(), calls=%async_computation.19 | async-start | bytes 589824
  350.8 136.7 %copy-start.13 = (f32[1024,32]{0,1:T(8,128)S(1)}, f32[1024,32]{0,1:T(8,128)}, u32[]{:S(2)}) copy-start(f32[1024,32]{0,1:T(8,128)} %copy-done.12) | copy-start | bytes 393220
  350.8 136.7 %copy-start.15 = (f32[1024,32]{0,1:T(8,128)S(1)}, f32[1024,32]{0,1:T(8,128)}, u32[]{:S(2)}) copy-start(f32[1024,32]{0,1:T(8,128)} %copy-done.14) | copy-start | bytes 393220
  354.6 1.3 copy-start.6
  355.9 3.6 copy-start
  420.9 1.3 copy-start.6
  422.2 5.0 copy-start
  487.4 131.0 %reduce-scatter.25.cloned.1.call-start = ((), (), s32[]{:S(2)}) async-start(), calls=%async_computation.18 | async-start | bytes 1769472
  489.1 1.9 copy-start.25
  490.8 3.1 copy-start.10
  493.9 2.8 copy-start.11
  496.7 154.8 %reduce-scatter.23.cloned.1.call-start = ((), (), s32[]{:S(2)}) async-start(), calls=%async_computation.17 | async-start | bytes 2621440 | tf_op jit(solution)/shard_map/reduce_scatter | solution.py:278
  501.3 191.2 %reduce-scatter.19.cloned.1.call-start = ((), (), s32[]{:S(2)}) async-start(), calls=%async_computation.13 | async-start | bytes 2621440 | tf_op jit(solution)/shard_map/reduce_scatter | solution.py:229
  506.3 145.2 %copy-start.19 = (f32[1024]{0:T(1024)S(1)}, f32[1024]{0:T(1024)}, u32[]{:S(2)}) copy-start(f32[1024]{0:T(1024)} %param.14) | copy-start | bytes 12292
  506.3 145.2 %copy-start.21 = (f32[256]{0:T(256)S(1)}, f32[256]{0:T(256)}, u32[]{:S(2)}) copy-start(f32[256]{0:T(256)} %copy-done.20) | copy-start | bytes 3076
  506.3 145.2 %copy-start.23 = (f32[256]{0:T(256)S(1)}, f32[256]{0:T(256)}, u32[]{:S(2)}) copy-start(f32[256]{0:T(256)} %copy-done.22) | copy-start | bytes 3076
  506.3 186.3 %copy-start.3 = (bf16[256,1024]{1,0:T(8,128)(2,1)S(1)}, bf16[256,1024]{1,0:T(8,128)(2,1)}, u32[]{:S(2)}) copy-start(bf16[256,1024]{1,0:T(8,128)(2,1)} %reduce-scatter.21.cloned.1.call-done) | copy-start | bytes 1572868
  506.3 186.3 %copy-start.5 = (bf16[256,1024]{1,0:T(8,128)(2,1)S(1)}, bf16[256,1024]{1,0:T(8,128)(2,1)}, u32[]{:S(2)}) copy-start(bf16[256,1024]{1,0:T(8,128)(2,1)} %param.21) | copy-start | bytes 1572868
  (1 other events, 0.6 us)
Sparse Core Ops, SparseCore 0:
  10.0 51.3 all-gather.8
  63.6 21.1 all-gather.6
  113.4 31.4 reduce-scatter.16
  147.0 57.6 all-gather.10
  206.7 40.7 all-gather.12
  249.1 21.2 all-gather.14
  284.1 31.4 reduce-scatter.20
  319.8 22.5 all-gather.16
  345.8 64.9 reduce-scatter.30
  414.6 71.0 reduce-scatter.28
  490.0 61.2 reduce-scatter.26
  554.5 63.8 reduce-scatter.24
  621.1 30.3 reduce-scatter.22
  653.9 31.4 reduce-scatter.18
